TPU v7x, 512 devices: a whole 4x8x8 slice. The times are simulated.
512 devices in a mesh: dp: 8 (over z_lo, core), ctx: 64 (over y, x, z_hi).
Axes of the slice: x: 4, y: 8, z: 8 (z_hi: 2, z_lo: 4; z = z_hi * 4 + z_lo), core: 2. Of those that a mesh axis runs over, the one named last changes fastest.
Arguments:
- queries: bfloat16 [65536, 1024], P(('dp', 'ctx')), parts along dimension 0, may hold values from -6 to 6
- keys: bfloat16 [65536, 256], P(('dp', 'ctx')), parts along dimension 0, may hold values from -6 to 6
- values: bfloat16 [65536, 256], P(('dp', 'ctx')), parts along dimension 0, may hold values from -6 to 6
- positions: int32 [65536], P(('dp', 'ctx')), parts along dimension 0, may hold values from 0 to 8191, as said below
Outputs:
- attended: bfloat16 [65536, 1024], P(('dp', 'ctx')), parts along dimension 0
- log_sum_exp: float32 [8, 65536], P(None, ('dp', 'ctx')), parts along dimension 1
There are 8 independent parts, one for each index of `dp`. A program takes and returns all parts, laid end to end along the dimension named above; each array names one. Nothing has to cross between parts.
Inputs may be any that keep to these rules, and one draw needn't show every extreme that they name: A permutation of the positions of one book; each index of ctx holds two runs of 64 consecutive positions, first run number c, then run number 2 * 64 - 1 - c, in units of 64 positions.
All inputs are finite; a program needn't handle non-finite values.
Results may differ from a plain program's by a relative error of at most 0.0055.
Values may be sent and summed in bfloat16 or wider, within the bound.
A program may use at most 64 MiB of HBM per device.

v0:
```python
import jax
import jax.numpy as jnp
from jax import lax
from jax.sharding import PartitionSpec as P

HD = 128
QH = 8
KVH = 2


def attend(carry, grouped, block_keys, block_values, block_pos, query_pos):
    maxima, totals, accumulated = carry
    count_rows = block_keys.shape[0]
    key_heads = block_keys.reshape(count_rows, KVH, HD)
    value_heads = block_values.reshape(count_rows, KVH, HD)
    scores = jnp.einsum(
        "qhgd,khd->hgqk", grouped, key_heads, preferred_element_type=jnp.float32
    ) * HD ** (-0.5)
    allowed = jnp.logical_and(query_pos[:, None] >= block_pos[None, :], True)
    scores = jnp.where(allowed, scores, -1e30)
    newest = jnp.maximum(maxima, jnp.max(scores, axis=-1))
    weights = jnp.where(allowed, jnp.exp(scores - newest[..., None]), 0.0)
    shrink = jnp.exp(maxima - newest)
    totals = totals * shrink + jnp.sum(weights, axis=-1)
    update = jnp.einsum(
        "hgqk,khd->hgqd",
        weights.astype(jnp.bfloat16),
        value_heads,
        preferred_element_type=jnp.float32,
    )
    accumulated = accumulated * shrink[..., None] + update
    return (newest, totals, accumulated)


def fold_rows(carry, grouped, piece, query_pos):
    block_keys, block_values, block_pos = piece
    count_rows = block_keys.shape[0]
    splits = count_rows // 512
    stacked = (
        block_keys.reshape(splits, 512, block_keys.shape[1]),
        block_values.reshape(splits, 512, block_values.shape[1]),
        block_pos.reshape(splits, 512),
    )

    def inner(state, blocks):
        return (attend(state, grouped, blocks[0], blocks[1], blocks[2], query_pos), None)

    carry, unused_out = lax.scan(inner, carry, stacked)
    return carry


def shards(queries, keys, values, positions):
    rows = queries.shape[0]
    groups = QH // KVH
    grouped = queries.reshape(rows, KVH, groups, HD)
    initial = (
        jnp.full((KVH, groups, rows), -1e30, jnp.float32),
        jnp.zeros((KVH, groups, rows), jnp.float32),
        jnp.zeros((KVH, groups, rows, HD), jnp.float32),
    )
    state = fold_rows(
        initial,
        grouped,
        (
            lax.all_gather(keys, "ctx", axis=0, tiled=True),
            lax.all_gather(values, "ctx", axis=0, tiled=True),
            lax.all_gather(positions, "ctx", axis=0, tiled=True),
        ),
        positions,
    )
    maxima, totals, accumulated = state
    output = accumulated / totals[..., None]
    attended = jnp.transpose(output, (2, 0, 1, 3)).reshape(rows, QH * HD).astype(jnp.bfloat16)
    log_sum_exp = (maxima + jnp.log(totals)).reshape(QH, rows)
    return (attended, log_sum_exp)


def solution(mesh):
    return jax.shard_map(
        shards,
        mesh=mesh,
        in_specs=(
            P(("dp", "ctx"), None),
            P(("dp", "ctx"), None),
            P(("dp", "ctx"), None),
            P(("dp", "ctx")),
        ),
        out_specs=(P(("dp", "ctx"), None), P(None, ("dp", "ctx"))),
        check_vma=False,
    )
```

profile of v0, /device:TPU:1, one launch (start us, length us, event | category | flops | bytes accessed | tf_op | source)
XLA Modules:
  0.0 407.6 jit_solution(4610863750571405695)
XLA Ops:
  7.2 0.7 all-gather.4.cloned.1.call-update
  7.9 0.7 all-gather.6.cloned.1.call-update
  8.7 199.5 %all-gather = s32[64,1,128]{2,1,0:T(1,128)S(1)} all-gather(s32[1,1,128]{2,1,0:T(1,128)} %bitcast.61), channel_id=1, replica_groups=mesh['dp'=8,'ctx'=64] {'ctx'}, dimensions={0}, use_global_device_ids=true | all-gather | bytes 33280 | tf_op jit(solution)/shard_map/all_gather | solution.py:67
  208.6 0.7 reduce.3
  209.4 1.1 copy.25
  210.7 119.6 %all-gather.6.cloned.1.call-done = bf16[8192,256]{1,0:T(8,128)(2,1)} async-done(((bf16[128,256]{1,0:T(8,128)(2,1)}), bf16[8192,256]{1,0:T(8,128)(2,1)}) %all-gather.6.cloned.1.call-update) | async-done | bytes 4194320 | tf_op jit(solution)/shard_map/all_gather | solution.py:66
  330.4 68.5 %while.15 = (s32[]{:T(128)}, f32[2,4,128]{2,1,0:T(4,128)S(1)}, f32[2,4,128]{2,1,0:T(4,128)S(1)}, f32[2,4,128,128]{3,2,1,0:T(8,128)S(1)}, s32[128]{0:T(128)}, /*i...) while((s32[]{:T(128)}, f32[2,4,128]{2,1,0:T(4,128)S(1)}, ...), condition=%wide.region_3.4_spmd.clone, body=%wide.region_0.3_spmd.clone.sunk | while | flops 275715072 | bytes 10558089 | solution.py:48
  330.4 0.8 broadcast_compare_fusion.2
  331.2 1.1 constant_dynamic-slice_fusion.6
  333.6 1.0 convolution_add_fusion.2
  334.7 0.8 broadcast_compare_fusion.2
  335.5 1.1 constant_dynamic-slice_fusion.6
  336.8 0.5 fusion.27
  337.9 1.0 convolution_add_fusion.2
  338.9 0.8 broadcast_compare_fusion.2
  339.7 1.1 constant_dynamic-slice_fusion.6
  342.2 1.0 convolution_add_fusion.2
  343.2 0.8 broadcast_compare_fusion.2
  344.0 1.1 constant_dynamic-slice_fusion.6
  345.4 0.5 fusion.27
  346.5 1.0 convolution_add_fusion.2
  347.5 0.8 broadcast_compare_fusion.2
  348.3 1.1 constant_dynamic-slice_fusion.6
  349.7 0.5 fusion.27
  350.8 1.0 convolution_add_fusion.2
  351.8 0.8 broadcast_compare_fusion.2
  352.6 1.1 constant_dynamic-slice_fusion.6
  355.0 1.0 convolution_add_fusion.2
  356.1 0.8 broadcast_compare_fusion.2
  356.9 1.1 constant_dynamic-slice_fusion.6
  359.3 1.0 convolution_add_fusion.2
  360.3 0.8 broadcast_compare_fusion.2
  361.1 1.1 constant_dynamic-slice_fusion.6
  362.5 0.5 fusion.27
  363.6 1.0 convolution_add_fusion.2
  364.6 0.8 broadcast_compare_fusion.2
  365.4 1.1 constant_dynamic-slice_fusion.6
  367.9 1.0 convolution_add_fusion.2
  368.9 0.8 broadcast_compare_fusion.2
  369.7 1.1 constant_dynamic-slice_fusion.6
  372.2 1.0 convolution_add_fusion.2
  373.2 0.8 broadcast_compare_fusion.2
  374.0 1.1 constant_dynamic-slice_fusion.6
  375.4 0.5 fusion.27
  376.5 1.0 convolution_add_fusion.2
  377.5 0.8 broadcast_compare_fusion.2
  378.3 1.1 constant_dynamic-slice_fusion.6
  380.7 1.0 convolution_add_fusion.2
  381.7 0.8 broadcast_compare_fusion.2
  382.5 1.1 constant_dynamic-slice_fusion.6
  383.9 0.5 fusion.27
  385.0 1.0 convolution_add_fusion.2
  386.0 0.8 broadcast_compare_fusion.2
  386.8 1.1 constant_dynamic-slice_fusion.6
  388.2 0.5 fusion.27
  389.3 1.0 convolution_add_fusion.2
  390.3 0.8 broadcast_compare_fusion.2
  391.1 1.1 constant_dynamic-slice_fusion.6
  393.6 1.0 convolution_add_fusion.2
  394.6 0.8 broadcast_compare_fusion.2
  395.4 1.1 constant_dynamic-slice_fusion.6
  397.9 1.0 convolution_add_fusion.2
  399.3 0.9 convert_element_type.14
  400.1 0.6 log_add_fusion
  (132 shorter events, 19.5 us)
Async XLA Ops:
  7.2 203.6 %all-gather.4.cloned.1.call-start = ((), (), s32[]{:S(2)}) async-start(), calls=%async_computation | async-start | bytes 4259840 | tf_op jit(solution)/shard_map/all_gather | solution.py:65
  7.9 322.5 %all-gather.6.cloned.1.call-start = ((), (), s32[]{:S(2)}) async-start(), calls=%async_computation.1 | async-start | bytes 4259840 | tf_op jit(solution)/shard_map/all_gather | solution.py:66
Sparse Core Ops, SparseCore 0:
  12.5 160.9 all-gather.3
  178.0 152.3 all-gather.5
where the time goes:
time: 411 us; the launch traced here: 408 us
  blocking collectives  199 us (48%)
  waiting for transfers between devices  121 us (29%)
  local copies, waits for them, and re-layouts  24.8 us (6%)
  matrix products  24.1 us (6%)
  other arithmetic  22.9 us (6%)
  between operations  14.1 us (3%)
    all_gather x1, blocking collectives, shards(): lax.all_gather(positions, 'ctx', axis=0, tiled=True)  199 us
    all_gather x1, waiting for transfers between devices, shards(): lax.all_gather(values, 'ctx', axis=0, tiled=True)  120 us
    dynamic_slice x64, local copies, waits for them, and re-layouts, fold_rows(): carry, unused_out = lax.scan(inner, carry, stacked)  21.8 us
    dot_general x16, matrix products, attend(): jnp.einsum('hgqk,khd->hgqd', weights.astype(jnp.bfloat16), value_heads, p...  15.5 us
    ge x16, other arithmetic, attend(): allowed = jnp.logical_and(query_pos[:, None] >= block_pos[None, :], True)  12.6 us
    dot_general x16, matrix products, attend(): jnp.einsum('qhgd,khd->hgqk', grouped, key_heads, preferred_element_type=j...  8.59 us
    reduce_sum x16, other arithmetic, attend(): totals = totals * shrink + jnp.sum(weights, axis=-1)  8.32 us
  transfers between devices with their start and end apart: 2, of which 1 were waited for; matrix products, arithmetic and copies ran while one was open for 1% of the time, Pallas kernels for 0%

commit v1 on v0

v1 whole, which is shorter than its diff:
```python
import functools
import math

import jax
import jax.numpy as jnp
from jax import lax
from jax.experimental import pallas as pl
from jax.experimental.pallas import tpu as pltpu
from jax.sharding import PartitionSpec as P

MESH = pl.DeviceIdType.MESH
F32 = jnp.float32
BF16 = jnp.bfloat16
HD = 128
QH = 8
KVH = 2
GROUP = QH // KVH
TOK = 128
RUN = 64
NX, NY, NZ = 4, 8, 2
SCALE = math.log2(math.e) / math.sqrt(HD)
NEG = -1e30
KV_ROWS = 4 * RUN
Q_ROWS = 2 * GROUP * RUN
META = 16
OWN, Z0 = 0, 1
OM = {0: OWN, 1: 2, 2: 4, 3: 8, 4: 12}
OP = {0: OWN, 1: 3, 2: 5, 3: 9, 4: 12}
ZM = {0: Z0, 1: 6, 2: 10, 3: 13, 4: 15}
ZP = {0: Z0, 1: 7, 2: 11, 3: 14, 4: 15}
SLOTS = 16
CHUNK = 4
X_STEP = {1: 1, 2: NX - 1, 3: 2}
X_BACK = {1: 2, 2: 1, 3: 3}


def nt(a, b):
    return lax.dot_general(a, b, (((1,), (1,)), ((), ())), preferred_element_type=F32)


def nn(a, b):
    return lax.dot_general(a, b, (((1,), (0,)), ((), ())), preferred_element_type=F32)


def lanes(x, n):
    return jnp.concatenate([x] * (n // HD), axis=1)


def fold(q, parts, m_ref, l_ref, a_ref, first):
    scores = []
    for k, unused_v, bias in parts:
        s = nt(q, k)
        scores.append(s if bias is None else s + bias)
    peak = functools.reduce(jnp.maximum, [jnp.max(s, axis=1, keepdims=True) for s in scores])
    if first:
        new = jnp.broadcast_to(peak, m_ref.shape)
    else:
        old = m_ref[...]
        new = jnp.maximum(old, peak)
    shift = new * SCALE
    total = None
    update = None
    for s, (unused_k, v, unused_bias) in zip(scores, parts):
        p = jnp.exp2(s * SCALE - lanes(shift, s.shape[1]))
        for i in range(s.shape[1] // HD):
            piece = p[:, i * HD : (i + 1) * HD]
            total = piece if total is None else total + piece
        pv = nn(p.astype(BF16), v)
        update = pv if update is None else update + pv
    if first:
        l_ref[...] = total
        a_ref[...] = update
    else:
        shrink = jnp.exp2(old * SCALE - shift)
        l_ref[...] = l_ref[...] * shrink + total
        a_ref[...] = a_ref[...] * shrink + update
    m_ref[...] = new


def kernel(
    pos_ref, q_ref, k_ref, v_ref, out_ref, lse_ref,
    kv, qb, ob, osend, m, l, a,
    kv_send, kv_recv, q_send, q_recv, o_send, o_recv,
):
    me = lax.axis_index("ctx")
    my_y, my_x, my_z = me // (NX * NZ), lax.rem(me // NZ, NX), lax.rem(me, NZ)

    def at(dy, dx, dz):
        y, x, z = lax.rem(my_y + dy, NY), lax.rem(my_x + dx, NX), lax.rem(my_z + dz, NZ)
        return {"ctx": (y * NX + x) * NZ + z}

    up, down, across = at(1, 0, 0), at(NY - 1, 0, 0), at(0, 0, 1)
    row = {i: at(0, X_STEP[i], 0) for i in (1, 2, 3)}
    barrier = pltpu.get_barrier_semaphore()
    for peer in (across, row[3], up, down, row[1], row[2]):
        pl.semaphore_signal(barrier, inc=1, device_id=peer, device_id_type=MESH)

    number = lax.shift_right_logical(pos_ref[...], 6)
    low = jnp.minimum(number, 2 * RUN - 1 - number)
    lane = lax.broadcasted_iota(jnp.int32, (1, HD), 1)
    swapped = jnp.where((low == number) == (lane < RUN), 0.0, 1.0)
    meta = jnp.broadcast_to(low.astype(F32), (META, HD)).astype(BF16)
    turn = jnp.broadcast_to(swapped, (RUN, HD)).astype(BF16) > 0.5

    def half(ref, r, cols):
        return jnp.where(turn, ref[(1 - r) * RUN : (2 - r) * RUN, cols], ref[r * RUN : (r + 1) * RUN, cols])

    def stage_kv(h):
        cols = slice(h * HD, (h + 1) * HD)
        for r in range(2):
            kv[h, OWN, r * RUN : (r + 1) * RUN, :] = half(k_ref, r, cols)
            kv[h, OWN, (2 + r) * RUN : (3 + r) * RUN, :] = half(v_ref, r, cols)
        if h == 0:
            kv[h, OWN, KV_ROWS:, :] = meta

    def stage_q(h):
        for r in range(2):
            for g in range(GROUP):
                base = (r * GROUP + g) * RUN
                cols = slice((h * GROUP + g) * HD, (h * GROUP + g + 1) * HD)
                qb[h, 0, base : base + RUN, :] = half(q_ref, r, cols)
        if h == 0:
            qb[h, 0, Q_ROWS:, :] = meta

    started = []

    def kv_copy(h, src, dst, device):
        n = KV_ROWS + (META if h == 0 else 0)
        return pltpu.make_async_remote_copy(
            src_ref=kv.at[h, src, 0:n], dst_ref=kv.at[h, dst, 0:n],
            send_sem=kv_send.at[h, dst], recv_sem=kv_recv.at[h, dst],
            device_id=device, device_id_type=MESH,
        )

    def send_kv(h, src, dst, device):
        copy = kv_copy(h, src, dst, device)
        copy.start()
        started.append(copy)

    def got_kv(h, slot):
        kv_copy(h, slot, slot, up).wait_recv()

    def q_copy(h, i):
        n = Q_ROWS + (META if h == 0 else 0)
        return pltpu.make_async_remote_copy(
            src_ref=qb.at[h, 0, 0:n], dst_ref=qb.at[h, X_BACK[i], 0:n],
            send_sem=q_send.at[h, i], recv_sem=q_recv.at[h, X_BACK[i]],
            device_id=row[i], device_id_type=MESH,
        )

    def o_copy(h, i):
        return pltpu.make_async_remote_copy(
            src_ref=osend.at[h, i], dst_ref=ob.at[h, X_BACK[i]],
            send_sem=o_send.at[h, i], recv_sem=o_recv.at[h, X_BACK[i]],
            device_id=row[i], device_id_type=MESH,
        )

    def ring(h, step, o_part, z_part):
        if step < NY // 2 - 1:
            both = ((OM, up), (OP, down)) if o_part else ((ZM, up), (ZP, down))
            for slots, device in both:
                if step > 0:
                    got_kv(h, slots[step])
                send_kv(h, slots[step], slots[step + 1], device)
        else:
            both = (OM, OP) if o_part else (ZM, ZP)
            for slots in both:
                got_kv(h, slots[step])
            slots, device = (both[0], up) if h == 0 else (both[1], down)
            send_kv(h, slots[step], slots[step + 1], device)

    stage_kv(0)
    stage_kv(1)
    stage_q(0)
    stage_q(1)
    pl.semaphore_wait(barrier, 6)
    for h in range(KVH):
        send_kv(h, OWN, Z0, across)
        ring(h, 0, True, False)
    for h in range(KVH):
        for i in (3, 1, 2):
            q_copy(h, i).start()

    lane64 = lane < RUN
    wide = CHUNK * RUN

    def attend(h, chunk):
        first = chunk == 0
        s0 = chunk * CHUNK
        block = [kv[h, s0 : s0 + CHUNK, i * RUN : (i + 1) * RUN, :].reshape(wide, HD) for i in range(4)]
        run = [kv[0, s0 + i, KV_ROWS : KV_ROWS + META, :].astype(F32)[0:1] for i in range(CHUNK)]
        theirs = jnp.concatenate(
            [jnp.where(lane64, run[i], run[i + 1]) for i in range(0, CHUNK, 2)], axis=1
        )
        for c in range(NX):
            mine = lanes(qb[0, c, Q_ROWS : Q_ROWS + META, :].astype(F32)[0:1], wide)
            bias1 = jnp.where(theirs < mine, 0.0, NEG)
            bias2 = jnp.where(theirs > mine, 0.0, NEG)
            if first and c == 0:
                token = lax.rem(lax.broadcasted_iota(jnp.int32, (GROUP * RUN, wide), 0), RUN)
                column = lax.broadcasted_iota(jnp.int32, (GROUP * RUN, wide), 1)
                bias1 = jnp.where(column <= token, 0.0, bias1)
                bias2 = jnp.where(column <= token, 0.0, bias2)
            q1 = qb[h, c, 0 : GROUP * RUN, :]
            q2 = qb[h, c, GROUP * RUN : Q_ROWS, :]
            k1, k2, v1, v2 = block
            fold(q2, [(k1, v1, None), (k2, v2, bias2)], m.at[h, c, 1], l.at[h, c, 1], a.at[h, c, 1], first)
            fold(q1, [(k1, v1, bias1)], m.at[h, c, 0], l.at[h, c, 0], a.at[h, c, 0], first)

    eye = lax.broadcasted_iota(jnp.int32, (HD, HD), 0) == lax.broadcasted_iota(jnp.int32, (HD, HD), 1)

    def close(h, c, dst):
        logs = []
        for r in range(2):
            total = jnp.sum(l[h, c, r], axis=1, keepdims=True)
            dst[r * GROUP * RUN : (r + 1) * GROUP * RUN, :] = (a[h, c, r] * (1.0 / total)).astype(BF16)
            logs.append(m[h, c, r] * SCALE + jnp.log2(total))
        rows = []
        for g in range(GROUP):
            both = jnp.concatenate([logs[r][g * RUN : (g + 1) * RUN] for r in range(2)], axis=0)
            rows.append(jnp.sum(jnp.where(eye, both, 0.0), axis=0, keepdims=True))
        rest = jnp.concatenate(rows, axis=0)
        pieces = []
        for unused in range(3):
            piece = rest.astype(BF16).astype(F32)
            rest = rest - piece
            pieces.append(piece)
        pieces.append(jnp.zeros_like(rest))
        dst[Q_ROWS:, :] = jnp.concatenate(pieces, axis=0).astype(BF16)

    def finish(h):
        for i in (3, 1, 2):
            close(h, i, osend.at[h, i])
            o_copy(h, i).start()
        close(h, 0, ob.at[h, 0])

    to_row = lax.broadcasted_iota(jnp.int32, (HD, HD), 0)
    from_row = lax.broadcasted_iota(jnp.int32, (HD, HD), 1)
    place = to_row == jnp.where(swapped > 0.5, lax.bitwise_xor(from_row, RUN), from_row)

    def merge(h):
        for i in (1, 2, 3):
            o_copy(h, i).wait_recv()
        logs = []
        for i in range(NX):
            t = ob[h, i, Q_ROWS:, :].astype(F32)
            logs.append(t[0:4] + t[4:8] + t[8:12])
        top = functools.reduce(jnp.maximum, logs)
        weights = [jnp.exp2(x - top) for x in logs]
        total = sum(weights[1:], weights[0])
        whole = (top + jnp.log2(total)) * math.log(2.0)
        turned = jnp.concatenate([whole[:, RUN:], whole[:, :RUN]], axis=1)
        lse_ref[h * GROUP : (h + 1) * GROUP, :] = jnp.where(swapped > 0.5, turned, whole)
        weights = [w / total for w in weights]
        for g in range(GROUP):
            left, right = [], []
            for i in range(NX):
                diagonal = jnp.where(place, weights[i][g : g + 1, :], 0.0)
                high = diagonal.astype(BF16)
                left += [high, (diagonal - high.astype(F32)).astype(BF16)]
                part = [ob[h, i, (r * GROUP + g) * RUN : (r * GROUP + g + 1) * RUN, :] for r in range(2)]
                right += part + part
            o = nn(jnp.concatenate(left, axis=1), jnp.concatenate(right, axis=0))
            cols = slice((h * GROUP + g) * HD, (h * GROUP + g + 1) * HD)
            out_ref[:, cols] = o.astype(BF16)

    def got_q(h):
        for i in (1, 2, 3):
            q_copy(h, i).wait_recv()

    for h in range(KVH):
        ring(h, 1, True, False)
    for h in range(KVH):
        got_kv(h, Z0)
        ring(h, 0, False, True)
    got_q(0)
    attend(0, 0)
    for h in range(KVH):
        ring(h, 2, True, False)
    for h in range(KVH):
        ring(h, 1, False, True)
    got_q(1)
    attend(1, 0)
    attend(0, 1)
    for h in range(KVH):
        ring(h, 3, True, False)
    for h in range(KVH):
        ring(h, 2, False, True)
    attend(1, 1)
    attend(0, 2)
    for h in range(KVH):
        got_kv(h, OM[4])
    for h in range(KVH):
        ring(h, 3, False, True)
    attend(1, 2)
    for h in range(KVH):
        got_kv(h, ZM[4])
        attend(h, 3)
        finish(h)
    for h in range(KVH):
        merge(h)
    for copy in started:
        copy.wait_send()
    for h in range(KVH):
        for i in (1, 2, 3):
            q_copy(h, i).wait_send()
            o_copy(h, i).wait_send()


def shards(queries, keys, values, positions):
    vmem = pl.BlockSpec(memory_space=pltpu.VMEM)
    state = (KVH, NX, 2, GROUP * RUN, HD)
    return pl.pallas_call(
        kernel,
        name="ring_attention",
        out_shape=(
            jax.ShapeDtypeStruct((TOK, QH * HD), BF16),
            jax.ShapeDtypeStruct((QH, TOK), F32),
        ),
        in_specs=[vmem, vmem, vmem, vmem],
        out_specs=(vmem, vmem),
        scratch_shapes=[
            pltpu.VMEM((KVH, SLOTS, KV_ROWS + META, HD), BF16),
            pltpu.VMEM((KVH, NX, Q_ROWS + META, HD), BF16),
            pltpu.VMEM((KVH, NX, Q_ROWS + META, HD), BF16),
            pltpu.VMEM((KVH, NX, Q_ROWS + META, HD), BF16),
            pltpu.VMEM(state, F32),
            pltpu.VMEM(state, F32),
            pltpu.VMEM(state, F32),
            pltpu.SemaphoreType.DMA((KVH, SLOTS)),
            pltpu.SemaphoreType.DMA((KVH, SLOTS)),
            pltpu.SemaphoreType.DMA((KVH, NX)),
            pltpu.SemaphoreType.DMA((KVH, NX)),
            pltpu.SemaphoreType.DMA((KVH, NX)),
            pltpu.SemaphoreType.DMA((KVH, NX)),
        ],
        compiler_params=pltpu.CompilerParams(
            collective_id=0, has_side_effects=True, vmem_limit_bytes=40 * 2**20
        ),
    )(positions.reshape(1, TOK), queries, keys, values)


def solution(mesh):
    return jax.shard_map(
        shards,
        mesh=mesh,
        in_specs=(
            P(("dp", "ctx"), None),
            P(("dp", "ctx"), None),
            P(("dp", "ctx"), None),
            P(("dp", "ctx")),
        ),
        out_specs=(P(("dp", "ctx"), None), P(None, ("dp", "ctx"))),
        check_vma=False,
    )
```

time: 411 us -> 62.4 us (0.15)
  the two profiles are of different devices: /device:TPU:1 before, /device:TPU:2 now
where the time goes in v1:
time: 62.4 us; the launch traced here: 62.1 us
  Pallas kernels  56.9 us (91%)
  local copies, waits for them, and re-layouts  4.57 us (7%)
  between operations  0.65 us (1%)
    pallas_call x1, Pallas kernels, shards(): pl.pallas_call(kernel, name='ring_attention', out_shape=(jax.ShapeDtypeSt...  56.9 us
    unnamed x10, local copies, waits for them, and re-layouts  4.57 us

profile of v1, /device:TPU:2, one launch (start us, length us, event | category | flops | bytes accessed | tf_op | source)
XLA Modules:
  0.0 62.1 jit_solution(15426762865799875038)
XLA Ops:
  0.6 0.0 copy-start.3
  0.6 0.6 %copy-done.3 = s32[128]{0:T(128)S(1)} copy-done((s32[128]{0:T(128)S(1)}, s32[128]{0:T(128)}, u32[]{:S(2)}) %copy-start.3) | copy-done | bytes 536
  1.3 0.0 copy-start
  1.3 0.9 %copy-done = bf16[128,1024]{1,0:T(8,128)(2,1)S(1)} copy-done((bf16[128,1024]{1,0:T(8,128)(2,1)S(1)}, bf16[128,1024]{1,0:T(8,128)(2,1)}, u32[]{:S(2)}) %copy-start) | copy-done | bytes 262168
  2.2 0.0 copy-start.1
  2.2 0.8 %copy-done.1 = bf16[128,256]{1,0:T(8,128)(2,1)S(1)} copy-done((bf16[128,256]{1,0:T(8,128)(2,1)S(1)}, bf16[128,256]{1,0:T(8,128)(2,1)}, u32[]{:S(2)}) %copy-start.1) | copy-done | bytes 65560
  3.1 0.0 copy-start.2
  3.1 0.8 %copy-done.2 = bf16[128,256]{1,0:T(8,128)(2,1)S(1)} copy-done((bf16[128,256]{1,0:T(8,128)(2,1)S(1)}, bf16[128,256]{1,0:T(8,128)(2,1)}, u32[]{:S(2)}) %copy-start.2) | copy-done | bytes 65560
  3.9 56.9 %ring_attention.1 = (bf16[128,1024]{1,0:T(8,128)(2,1)S(1)}, f32[8,128]{1,0:T(8,128)S(1)}) custom-call(s32[1,128]{1,0:T(1,128)S(1)} %bitcast.1, bf16[128,1024]{1,0:T(8,128)(2,1)S(1)} %copy-done, bf16[128,256]{1,0:T(8,128)(2,1)S(1)} %copy-done.1, bf16[128,256]{1,0:T(8,128)(2,1)S(1)} %copy-done.2), custom_call_target="tpu_custom_call" | custom-call | tf_op jit(solution)/shard_map/ring_attention/pallas_call | solution.py:313
  60.8 0.7 %copy.8 = bf16[128,1024]{1,0:T(8,128)(2,1)} copy(bf16[128,1024]{1,0:T(8,128)(2,1)S(1)} %get-tuple-element.4) | data formatting | bytes 524288
  61.5 0.6 copy.9
Async XLA Ops:
  0.6 0.7 %copy-start.3 = (s32[128]{0:T(128)S(1)}, s32[128]{0:T(128)}, u32[]{:S(2)}) copy-start(s32[128]{0:T(128)} %param.7) | copy-start | bytes 1540
  1.3 0.9 %copy-start = (bf16[128,1024]{1,0:T(8,128)(2,1)S(1)}, bf16[128,1024]{1,0:T(8,128)(2,1)}, u32[]{:S(2)}) copy-start(bf16[128,1024]{1,0:T(8,128)(2,1)} %q_ref.1) | copy-start | bytes 786436
  2.2 0.8 %copy-start.1 = (bf16[128,256]{1,0:T(8,128)(2,1)S(1)}, bf16[128,256]{1,0:T(8,128)(2,1)}, u32[]{:S(2)}) copy-start(bf16[128,256]{1,0:T(8,128)(2,1)} %k_ref.1) | copy-start | bytes 196612
  3.1 0.8 %copy-start.2 = (bf16[128,256]{1,0:T(8,128)(2,1)S(1)}, bf16[128,256]{1,0:T(8,128)(2,1)}, u32[]{:S(2)}) copy-start(bf16[128,256]{1,0:T(8,128)(2,1)} %v_ref.1) | copy-start | bytes 196612

commit v2 on v1

v2 whole, which is shorter than its diff:
```python
import functools
import math

import jax
import jax.numpy as jnp
from jax import lax
from jax.experimental import pallas as pl
from jax.experimental.pallas import tpu as pltpu
from jax.sharding import PartitionSpec as P

MESH = pl.DeviceIdType.MESH
F32 = jnp.float32
BF16 = jnp.bfloat16
HD = 128
QH = 8
KVH = 2
GROUP = QH // KVH
TOK = 128
RUN = 64
NX, NY, NZ = 4, 8, 2
SCALE = math.log2(math.e) / math.sqrt(HD)
NEG = -1e6
KV_ROWS = 4 * RUN
Q_ROWS = 2 * GROUP * RUN
META = 16
CHUNKS = (
    (("OO", 0), ("OX", 0), ("OO", -1), ("OO", 1)),
    (("OX", -1), ("OX", 1), ("OO", -2), ("OO", 2)),
    (("OX", -2), ("OX", 2), ("ZO", 0), ("ZX", 0)),
    (("OO", -3), ("OO", 3), ("OX", -3), ("OX", 3)),
    (("ZO", -1), ("ZO", 1), ("ZX", -1), ("ZX", 1)),
    (("OO", 4), ("OX", 4), ("ZO", -2), ("ZO", 2)),
    (("ZX", -2), ("ZX", 2)),
    (("ZO", -3), ("ZO", 3), ("ZX", -3), ("ZX", 3)),
    (("ZO", 4), ("ZX", 4)),
)
FIRST = [sum(len(chunk) for chunk in CHUNKS[:i]) for i in range(len(CHUNKS))]
SLOT = {name: i for i, name in enumerate(name for chunk in CHUNKS for name in chunk)}
PLAN = (
    ("pass", "OO", 1), ("pass", "OX", 1),
    ("pass", "OO", 2), ("pass", "OX", 2),
    ("pass", "ZO", 0), ("pass", "ZX", 0), ("query",), ("wait", "OX", 0), ("attend", 0), ("attend", 1),
    ("pass", "OO", 3), ("pass", "OX", 3),
    ("pass", "ZO", 1), ("pass", "ZX", 1), ("attend", 2),
    ("far", "OO"), ("far", "OX"), ("attend", 3),
    ("pass", "ZO", 2), ("pass", "ZX", 2), ("attend", 4), ("attend", 5), ("attend", 6),
    ("wait", "ZO", 3), ("wait", "ZX", 3), ("attend", 7), ("wait", "ZO", 4), ("wait", "ZX", 4), ("attend", 8),
)
X_STEP = {1: 1, 2: NX - 1, 3: 2}
X_BACK = {1: 2, 2: 1, 3: 3}


def nt(a, b):
    return lax.dot_general(a, b, (((1,), (1,)), ((), ())), preferred_element_type=F32)


def nn(a, b):
    return lax.dot_general(a, b, (((1,), (0,)), ((), ())), preferred_element_type=F32)


def lanes(x, n):
    return jnp.concatenate([x] * (n // HD), axis=1)


def fold(q, k, v, bias, m_ref, l_ref, a_ref, first):
    s = nt(q, k)
    if bias.shape[0] == 1:
        bias = jnp.broadcast_to(bias, (GROUP * RUN, bias.shape[1]))
    masked = s[: GROUP * RUN] + bias
    s = masked if s.shape[0] == GROUP * RUN else jnp.concatenate([masked, s[GROUP * RUN :]], axis=0)
    peak = jnp.max(s, axis=1, keepdims=True)
    if first:
        new = jnp.broadcast_to(peak, m_ref.shape)
    else:
        old = m_ref[...]
        new = jnp.maximum(old, peak)
    shift = new * SCALE
    p = jnp.exp2(s * SCALE - lanes(shift, s.shape[1]))
    total = sum((p[:, i : i + HD] for i in range(HD, s.shape[1], HD)), p[:, :HD])
    update = nn(p.astype(BF16), v)
    if first:
        l_ref[...] = total
        a_ref[...] = update
    else:
        shrink = jnp.exp2(old * SCALE - shift)
        l_ref[...] = l_ref[...] * shrink + total
        a_ref[...] = a_ref[...] * shrink + update
    m_ref[...] = new


def kernel(
    pos_ref, q_hbm, k_hbm, v_hbm, out_ref, lse_ref,
    q_ref, k_ref, v_ref, kv, spare, qb, qspare, ob, osend, m, l, a,
    load_sem, kv_send, kv_recv, q_send, q_recv, o_send, o_recv,
):
    loads = [
        pltpu.make_async_copy(src, dst, load_sem.at[i])
        for i, (src, dst) in enumerate(((k_hbm, k_ref), (v_hbm, v_ref), (q_hbm, q_ref)))
    ]
    for load in loads:
        load.start()
    me = lax.axis_index("ctx")
    my_y, my_x, my_z = me // (NX * NZ), lax.rem(me // NZ, NX), lax.rem(me, NZ)
    head = lax.rem(my_x, 2)
    pair_step = 1 + head * (NX - 2)

    def at(dy, dx, dz):
        y, x, z = lax.rem(my_y + dy, NY), lax.rem(my_x + dx, NX), lax.rem(my_z + dz, NZ)
        return {"ctx": (y * NX + x) * NZ + z}

    up, down, across = at(1, 0, 0), at(NY - 1, 0, 0), at(0, 0, 1)
    beside, diagonal = at(0, pair_step, 0), at(0, pair_step, 1)
    above, below = at(1, pair_step, 0), at(NY - 1, pair_step, 0)
    row = {i: at(0, X_STEP[i], 0) for i in (1, 2, 3)}
    barrier = pltpu.get_barrier_semaphore()
    greet = (diagonal, across, row[3], above, below, up, down, row[1], row[2])
    for peer in greet:
        pl.semaphore_signal(barrier, inc=1, device_id=peer, device_id_type=MESH)

    number = lax.shift_right_logical(pos_ref[...], 6)
    low = jnp.minimum(number, 2 * RUN - 1 - number)
    lane = lax.broadcasted_iota(jnp.int32, (1, HD), 1)
    swapped = jnp.where((low == number) == (lane < RUN), 0.0, 1.0)
    meta = jnp.broadcast_to(low.astype(F32), (META, HD)).astype(BF16)
    turn = jnp.broadcast_to(swapped, (RUN, HD)).astype(BF16) > 0.5

    def columns(h, g, heads):
        return pl.ds(pl.multiple_of((h * heads + g) * HD, HD), HD)

    def half(ref, r, cols):
        return jnp.where(turn, ref[(1 - r) * RUN : (2 - r) * RUN, cols], ref[r * RUN : (r + 1) * RUN, cols])

    def stage_kv(h, dst):
        cols = columns(h, 0, 1)
        for r in range(2):
            dst[r * RUN : (r + 1) * RUN, :] = half(k_ref, r, cols)
            dst[(2 + r) * RUN : (3 + r) * RUN, :] = half(v_ref, r, cols)
        dst[KV_ROWS:, :] = meta

    def stage_q(h, dst):
        for r in range(2):
            for g in range(GROUP):
                base = (r * GROUP + g) * RUN
                dst[base : base + RUN, :] = half(q_ref, r, columns(h, g, GROUP))
        dst[Q_ROWS:, :] = meta

    started = []

    def kv_copy(src, slot, device):
        return pltpu.make_async_remote_copy(
            src_ref=src, dst_ref=kv.at[slot], send_sem=kv_send.at[slot], recv_sem=kv_recv.at[slot],
            device_id=device, device_id_type=MESH,
        )

    def send_kv(src, name, device):
        copy = kv_copy(src, SLOT[name], device)
        copy.start()
        started.append(copy)

    def got_kv(*name):
        if name != ("OO", 0):
            kv_copy(kv.at[SLOT[name]], SLOT[name], up).wait_recv()

    def pass_on(stream, step):
        for y, device in ((-step, up), (step, down)):
            if step or device is up:
                got_kv(stream, y)
            after = y - 1 if device is up else y + 1
            block = kv.at[SLOT[stream, y]]
            if step < 3:
                send_kv(block, (stream, after), device)
            elif stream == ("OO" if device is up else "OX"):
                send_kv(block, (stream, 4), device)

    def far(stream):
        got_kv(stream, 4)
        send_kv(kv.at[SLOT[stream, 4]], ("Z" + stream[1], 4), across)

    def wait(stream, step):
        for y in (-step, step) if 0 < step < 4 else (step,):
            got_kv(stream, y)

    def q_copy(i):
        return pltpu.make_async_remote_copy(
            src_ref=qb.at[0] if i == 3 else qspare, dst_ref=qb.at[X_BACK[i]],
            send_sem=q_send.at[i], recv_sem=q_recv.at[X_BACK[i]],
            device_id=row[i], device_id_type=MESH,
        )

    def o_copy(i):
        return pltpu.make_async_remote_copy(
            src_ref=osend.at[i], dst_ref=ob.at[X_BACK[i]],
            send_sem=o_send.at[i], recv_sem=o_recv.at[X_BACK[i]],
            device_id=row[i], device_id_type=MESH,
        )

    lane64 = lane < RUN

    def attend(chunk):
        first = chunk == 0
        s0, size = FIRST[chunk], len(CHUNKS[chunk])
        wide = size * RUN
        k1, k2, v1, v2 = [
            kv[s0 : s0 + size, i * RUN : (i + 1) * RUN, :].reshape(wide, HD) for i in range(4)
        ]
        run = [kv[s0 + i, KV_ROWS:, :].astype(F32)[0:1] for i in range(size)]
        theirs = jnp.concatenate(
            [jnp.where(lane64, run[i], run[i + 1]) for i in range(0, size, 2)], axis=1
        )
        token = lax.rem(lax.broadcasted_iota(jnp.int32, (GROUP * RUN, wide), 0), RUN)
        column = lax.rem(lax.broadcasted_iota(jnp.int32, (GROUP * RUN, wide), 1), RUN)
        triangle = jnp.where(column <= token, 0.0, NEG)
        for c in range(NX):
            mine = lanes(qb[c, Q_ROWS:, :].astype(F32)[0:1], wide)
            bias1 = jnp.where(theirs < mine, 0.0, NEG)
            bias2 = jnp.where(theirs > mine, 0.0, NEG)
            if first and c < 3:
                bias1 = jnp.where(theirs == mine, triangle, bias1)
                bias2 = jnp.where(theirs == mine, triangle, bias2)
            second = slice(GROUP * RUN, Q_ROWS)
            fold(qb[c, :Q_ROWS, :], k1, v1, bias1, m.at[c], l.at[c], a.at[c], first)
            fold(qb[c, second, :], k2, v2, bias2, m.at[c, second], l.at[c, second], a.at[c, second], False)

    eye = lax.broadcasted_iota(jnp.int32, (HD, HD), 0) == lax.broadcasted_iota(jnp.int32, (HD, HD), 1)

    def close(c, dst):
        total = jnp.sum(l[c], axis=1, keepdims=True)
        dst[:Q_ROWS, :] = (a[c] * (1.0 / total)).astype(BF16)
        logs = m[c] * SCALE + jnp.log2(total)
        rows = []
        for g in range(GROUP):
            starts = [(r * GROUP + g) * RUN for r in range(2)]
            both = jnp.concatenate([logs[i : i + RUN] for i in starts], axis=0)
            rows.append(jnp.sum(jnp.where(eye, both, 0.0), axis=0, keepdims=True))
        rest = jnp.concatenate(rows, axis=0)
        pieces = []
        for unused in range(3):
            piece = rest.astype(BF16).astype(F32)
            rest = rest - piece
            pieces.append(piece)
        pieces.append(jnp.zeros_like(rest))
        dst[Q_ROWS:, :] = jnp.concatenate(pieces, axis=0).astype(BF16)

    to_row = lax.broadcasted_iota(jnp.int32, (HD, HD), 0)
    from_row = lax.broadcasted_iota(jnp.int32, (HD, HD), 1)
    place = to_row == jnp.where(swapped > 0.5, lax.bitwise_xor(from_row, RUN), from_row)

    def merge(h, sources):
        logs = []
        for i in sources:
            t = ob[i, Q_ROWS:, :].astype(F32)
            logs.append(t[0:4] + t[4:8] + t[8:12])
        top = functools.reduce(jnp.maximum, logs)
        weights = [jnp.exp2(x - top) for x in logs]
        total = sum(weights[1:], weights[0])
        weights = [w / total for w in weights]
        for g in range(GROUP):
            left, right = [], []
            for w, i in zip(weights, sources):
                spread = jnp.where(place, w[g : g + 1, :], 0.0)
                high = spread.astype(BF16)
                left += [high, (spread - high.astype(F32)).astype(BF16)]
                part = [ob[i, (r * GROUP + g) * RUN : (r * GROUP + g + 1) * RUN, :] for r in range(2)]
                right += part + part
            o = nn(jnp.concatenate(left, axis=1), jnp.concatenate(right, axis=0))
            out_ref[:, columns(h, g, GROUP)] = o.astype(BF16)
        whole = (top + jnp.log2(total)) * math.log(2.0)
        turned = jnp.concatenate([whole[:, RUN:], whole[:, :RUN]], axis=1)
        return jnp.where(swapped > 0.5, turned, whole)

    own = kv.at[SLOT["OO", 0]]
    loads[0].wait()
    loads[1].wait()
    stage_kv(head, own)
    stage_kv(1 - head, spare)
    loads[2].wait()
    stage_q(1 - head, qspare)
    stage_q(head, qb.at[0])
    pl.semaphore_wait(barrier, len(greet))
    send_kv(own, ("ZO", 0), across)
    send_kv(spare, ("ZX", 0), diagonal)
    send_kv(own, ("OO", -1), up)
    send_kv(own, ("OO", 1), down)
    send_kv(spare, ("OX", 0), beside)
    send_kv(spare, ("OX", -1), above)
    send_kv(spare, ("OX", 1), below)
    for i in (3, 1, 2):
        q_copy(i).start()
    for what, *rest in PLAN:
        if what == "query":
            for i in (1, 2, 3):
                q_copy(i).wait_recv()
        else:
            {"pass": pass_on, "far": far, "wait": wait, "attend": attend}[what](*rest)
    for i in (3, 1, 2):
        close(i, osend.at[i])
        o_copy(i).start()
    close(0, ob.at[0])
    o_copy(3).wait_recv()
    mine = merge(head, (0, 3))
    o_copy(1).wait_recv()
    o_copy(2).wait_recv()
    other = merge(1 - head, (1, 2))
    even = jnp.where(head == 0, 1.0, 0.0)
    lse_ref[0:GROUP, :] = jnp.where(even > 0.5, mine, other)
    lse_ref[GROUP:, :] = jnp.where(even > 0.5, other, mine)
    for copy in started:
        copy.wait_send()
    for i in (1, 2, 3):
        q_copy(i).wait_send()
        o_copy(i).wait_send()


def shards(queries, keys, values, positions):
    vmem = pl.BlockSpec(memory_space=pltpu.VMEM)
    hbm = pl.BlockSpec(memory_space=pltpu.HBM)
    state = pltpu.VMEM((NX, Q_ROWS, HD), F32)
    shared = pltpu.VMEM((NX, Q_ROWS + META, HD), BF16)
    blocks = len(SLOT)
    return pl.pallas_call(
        kernel,
        name="ring_attention",
        out_shape=(
            jax.ShapeDtypeStruct((TOK, QH * HD), BF16),
            jax.ShapeDtypeStruct((QH, TOK), F32),
        ),
        in_specs=[vmem, hbm, hbm, hbm],
        out_specs=(vmem, vmem),
        scratch_shapes=[
            pltpu.VMEM((TOK, QH * HD), BF16),
            pltpu.VMEM((TOK, KVH * HD), BF16),
            pltpu.VMEM((TOK, KVH * HD), BF16),
            pltpu.VMEM((blocks, KV_ROWS + META, HD), BF16),
            pltpu.VMEM((KV_ROWS + META, HD), BF16),
            shared,
            pltpu.VMEM((Q_ROWS + META, HD), BF16),
            shared,
            shared,
            state,
            state,
            state,
            pltpu.SemaphoreType.DMA((3,)),
            pltpu.SemaphoreType.DMA((blocks,)),
            pltpu.SemaphoreType.DMA((blocks,)),
            pltpu.SemaphoreType.DMA((NX,)),
            pltpu.SemaphoreType.DMA((NX,)),
            pltpu.SemaphoreType.DMA((NX,)),
            pltpu.SemaphoreType.DMA((NX,)),
        ],
        compiler_params=pltpu.CompilerParams(
            collective_id=0, has_side_effects=True, vmem_limit_bytes=40 * 2**20
        ),
    )(positions.reshape(1, TOK), queries, keys, values)


def solution(mesh):
    return jax.shard_map(
        shards,
        mesh=mesh,
        in_specs=(
            P(("dp", "ctx"), None),
            P(("dp", "ctx"), None),
            P(("dp", "ctx"), None),
            P(("dp", "ctx")),
        ),
        out_specs=(P(("dp", "ctx"), None), P(None, ("dp", "ctx"))),
        check_vma=False,
    )
```

time: 62.4 us -> 56.1 us (0.90)
  the two profiles are of different devices: /device:TPU:2 before, /device:TPU:1 now
where the time goes in v2:
time: 56.1 us; the launch traced here: 55.8 us
  Pallas kernels  50.6 us (90%)
  local copies, waits for them, and re-layouts  4.57 us (8%)
  between operations  0.65 us (1%)
    pallas_call x1, Pallas kernels, shards(): pl.pallas_call(kernel, name='ring_attention', out_shape=(jax.ShapeDtypeSt...  50.6 us
    unnamed x10, local copies, waits for them, and re-layouts  4.57 us

profile of v2, /device:TPU:1, one launch (start us, length us, event | category | flops | bytes accessed | tf_op | source)
XLA Modules:
  0.0 55.8 jit_solution(14848412932012530971)
XLA Ops:
  0.6 0.0 copy-start.3
  0.6 0.6 %copy-done.3 = s32[128]{0:T(128)S(1)} copy-done((s32[128]{0:T(128)S(1)}, s32[128]{0:T(128)}, u32[]{:S(2)}) %copy-start.3) | copy-done | bytes 536
  1.3 0.0 copy-start
  1.3 0.9 %copy-done = bf16[128,1024]{1,0:T(8,128)(2,1)S(1)} copy-done((bf16[128,1024]{1,0:T(8,128)(2,1)S(1)}, bf16[128,1024]{1,0:T(8,128)(2,1)}, u32[]{:S(2)}) %copy-start) | copy-done | bytes 262168
  2.2 0.0 copy-start.1
  2.2 0.8 %copy-done.1 = bf16[128,256]{1,0:T(8,128)(2,1)S(1)} copy-done((bf16[128,256]{1,0:T(8,128)(2,1)S(1)}, bf16[128,256]{1,0:T(8,128)(2,1)}, u32[]{:S(2)}) %copy-start.1) | copy-done | bytes 65560
  3.1 0.0 copy-start.2
  3.1 0.8 %copy-done.2 = bf16[128,256]{1,0:T(8,128)(2,1)S(1)} copy-done((bf16[128,256]{1,0:T(8,128)(2,1)S(1)}, bf16[128,256]{1,0:T(8,128)(2,1)}, u32[]{:S(2)}) %copy-start.2) | copy-done | bytes 65560
  3.9 50.6 %ring_attention.1 = (bf16[128,1024]{1,0:T(8,128)(2,1)S(1)}, f32[8,128]{1,0:T(8,128)S(1)}) custom-call(s32[1,128]{1,0:T(1,128)S(1)} %bitcast.1, bf16[128,1024]{1,0:T(8,128)(2,1)S(1)} %copy-done, bf16[128,256]{1,0:T(8,128)(2,1)S(1)} %copy-done.1, bf16[128,256]{1,0:T(8,128)(2,1)S(1)} %copy-done.2), custom_call_target="tpu_custom_call" | custom-call | tf_op jit(solution)/shard_map/ring_attention/pallas_call | solution.py:320
  54.5 0.7 %copy.8 = bf16[128,1024]{1,0:T(8,128)(2,1)} copy(bf16[128,1024]{1,0:T(8,128)(2,1)S(1)} %get-tuple-element.4) | data formatting | bytes 524288
  55.2 0.6 %copy.9 = f32[8,128]{1,0:T(8,128)} copy(f32[8,128]{1,0:T(8,128)S(1)} %get-tuple-element.5) | data formatting | bytes 8192
Async XLA Ops:
  0.6 0.7 %copy-start.3 = (s32[128]{0:T(128)S(1)}, s32[128]{0:T(128)}, u32[]{:S(2)}) copy-start(s32[128]{0:T(128)} %param.7) | copy-start | bytes 1540
  1.3 0.9 %copy-start = (bf16[128,1024]{1,0:T(8,128)(2,1)S(1)}, bf16[128,1024]{1,0:T(8,128)(2,1)}, u32[]{:S(2)}) copy-start(bf16[128,1024]{1,0:T(8,128)(2,1)} %q_hbm.1) | copy-start | bytes 786436
  2.2 0.8 %copy-start.1 = (bf16[128,256]{1,0:T(8,128)(2,1)S(1)}, bf16[128,256]{1,0:T(8,128)(2,1)}, u32[]{:S(2)}) copy-start(bf16[128,256]{1,0:T(8,128)(2,1)} %k_hbm.1) | copy-start | bytes 196612
  3.1 0.8 %copy-start.2 = (bf16[128,256]{1,0:T(8,128)(2,1)S(1)}, bf16[128,256]{1,0:T(8,128)(2,1)}, u32[]{:S(2)}) copy-start(bf16[128,256]{1,0:T(8,128)(2,1)} %v_hbm.1) | copy-start | bytes 196612

commit v3 on v2

--- a/solution.py
+++ b/solution.py
@@ -44,8 +44,9 @@
     ("pass", "ZO", 1), ("pass", "ZX", 1), ("attend", 2),
     ("far", "OO"), ("far", "OX"), ("attend", 3),
     ("pass", "ZO", 2), ("pass", "ZX", 2), ("attend", 4), ("attend", 5), ("attend", 6),
-    ("wait", "ZO", 3), ("wait", "ZX", 3), ("attend", 7), ("wait", "ZO", 4), ("wait", "ZX", 4), ("attend", 8),
+    ("wait", "ZO", 3), ("wait", "ZX", 3), ("wait", "ZO", 4), ("wait", "ZX", 4),
 )
+LAST = (7, 8)
 X_STEP = {1: 1, 2: NX - 1, 3: 2}
 X_BACK = {1: 2, 2: 1, 3: 3}
 
@@ -89,13 +90,13 @@
 
 
 def kernel(
-    pos_ref, q_hbm, k_hbm, v_hbm, out_ref, lse_ref,
-    q_ref, k_ref, v_ref, kv, spare, qb, qspare, ob, osend, m, l, a,
+    pos_hbm, q_hbm, k_hbm, v_hbm, out_ref, lse_ref,
+    pos_ref, q_ref, k_ref, v_ref, kv, spare, qb, qspare, ob, osend, m, l, a,
     load_sem, kv_send, kv_recv, q_send, q_recv, o_send, o_recv,
 ):
     loads = [
         pltpu.make_async_copy(src, dst, load_sem.at[i])
-        for i, (src, dst) in enumerate(((k_hbm, k_ref), (v_hbm, v_ref), (q_hbm, q_ref)))
+        for i, (src, dst) in enumerate(((k_hbm, k_ref), (v_hbm, v_ref), (q_hbm, q_ref), (pos_hbm, pos_ref)))
     ]
     for load in loads:
         load.start()
@@ -117,6 +118,7 @@
     for peer in greet:
         pl.semaphore_signal(barrier, inc=1, device_id=peer, device_id_type=MESH)
 
+    loads[3].wait()
     number = lax.shift_right_logical(pos_ref[...], 6)
     low = jnp.minimum(number, 2 * RUN - 1 - number)
     lane = lax.broadcasted_iota(jnp.int32, (1, HD), 1)
@@ -196,7 +198,7 @@
 
     lane64 = lane < RUN
 
-    def attend(chunk):
+    def attend(chunk, slots=range(NX)):
         first = chunk == 0
         s0, size = FIRST[chunk], len(CHUNKS[chunk])
         wide = size * RUN
@@ -210,7 +212,7 @@
         token = lax.rem(lax.broadcasted_iota(jnp.int32, (GROUP * RUN, wide), 0), RUN)
         column = lax.rem(lax.broadcasted_iota(jnp.int32, (GROUP * RUN, wide), 1), RUN)
         triangle = jnp.where(column <= token, 0.0, NEG)
-        for c in range(NX):
+        for c in slots:
             mine = lanes(qb[c, Q_ROWS:, :].astype(F32)[0:1], wide)
             bias1 = jnp.where(theirs < mine, 0.0, NEG)
             bias2 = jnp.where(theirs > mine, 0.0, NEG)
@@ -292,10 +294,14 @@
                 q_copy(i).wait_recv()
         else:
             {"pass": pass_on, "far": far, "wait": wait, "attend": attend}[what](*rest)
-    for i in (3, 1, 2):
-        close(i, osend.at[i])
-        o_copy(i).start()
-    close(0, ob.at[0])
+    for i in (3, 1, 2, 0):
+        for chunk in LAST:
+            attend(chunk, (i,))
+        if i:
+            close(i, osend.at[i])
+            o_copy(i).start()
+        else:
+            close(0, ob.at[0])
     o_copy(3).wait_recv()
     mine = merge(head, (0, 3))
     o_copy(1).wait_recv()
@@ -317,6 +323,7 @@
     state = pltpu.VMEM((NX, Q_ROWS, HD), F32)
     shared = pltpu.VMEM((NX, Q_ROWS + META, HD), BF16)
     blocks = len(SLOT)
+    inputs = (positions.reshape(1, TOK), queries, keys, values)
     return pl.pallas_call(
         kernel,
         name="ring_attention",
@@ -324,9 +331,10 @@
             jax.ShapeDtypeStruct((TOK, QH * HD), BF16),
             jax.ShapeDtypeStruct((QH, TOK), F32),
         ),
-        in_specs=[vmem, hbm, hbm, hbm],
+        in_specs=[hbm, hbm, hbm, hbm],
         out_specs=(vmem, vmem),
         scratch_shapes=[
+            pltpu.VMEM((1, TOK), jnp.int32),
             pltpu.VMEM((TOK, QH * HD), BF16),
             pltpu.VMEM((TOK, KVH * HD), BF16),
             pltpu.VMEM((TOK, KVH * HD), BF16),
@@ -339,7 +347,7 @@
             state,
             state,
             state,
-            pltpu.SemaphoreType.DMA((3,)),
+            pltpu.SemaphoreType.DMA((4,)),
             pltpu.SemaphoreType.DMA((blocks,)),
             pltpu.SemaphoreType.DMA((blocks,)),
             pltpu.SemaphoreType.DMA((NX,)),
@@ -350,7 +358,7 @@
         compiler_params=pltpu.CompilerParams(
             collective_id=0, has_side_effects=True, vmem_limit_bytes=40 * 2**20
         ),
-    )(positions.reshape(1, TOK), queries, keys, values)
+    )(*(pltpu.with_memory_space_constraint(x, pltpu.HBM) for x in inputs))
 
 
 def solution(mesh):

time: 56.1 us -> 50.7 us (0.904)
  local copies, waits for them, and re-layouts: 4.57 us -> 1.3 us
  Pallas kernels: 50.6 us -> 48.6 us
    unnamed x10 -> x2, local copies, waits for them, and re-layouts: 4.57 us -> 1.3 us
    pallas_call x1, Pallas kernels: 50.6 us -> 48.6 us  [shards(): pl.pallas_call(kernel, name='ring_attention', out_shape=(jax.ShapeDtypeSt...]
where the time goes in v3:
time: 50.7 us; the launch traced here: 50.5 us
  Pallas kernels  48.6 us (96%)
  local copies, waits for them, and re-layouts  1.3 us (3%)
  between operations  0.64 us (1%)
    pallas_call x1, Pallas kernels, shards(): pl.pallas_call(kernel, name='ring_attention', out_shape=(jax.ShapeDtypeSt...  48.6 us
    unnamed x2, local copies, waits for them, and re-layouts  1.3 us

profile of v3, /device:TPU:1, one launch (start us, length us, event | category | flops | bytes accessed | tf_op | source)
XLA Modules:
  0.0 50.5 jit_solution(15536550379739529236)
XLA Ops:
  0.6 48.6 %ring_attention.1 = (bf16[128,1024]{1,0:T(8,128)(2,1)S(1)}, f32[8,128]{1,0:T(8,128)S(1)}) custom-call(s32[1,128]{1,0:T(1,128)} %bitcast.1, bf16[128,1024]{1,0:T(8,128)(2,1)} %q_hbm.1, bf16[128,256]{1,0:T(8,128)(2,1)} %k_hbm.1, bf16[128,256]{1,0:T(8,128)(2,1)} %v_hbm.1), custom_call_target="tpu_custom_call" | custom-call | tf_op jit(solution)/shard_map/ring_attention/pallas_call | solution.py:327
  49.2 0.7 %copy.8 = bf16[128,1024]{1,0:T(8,128)(2,1)} copy(bf16[128,1024]{1,0:T(8,128)(2,1)S(1)} %get-tuple-element.4) | data formatting | bytes 524288
  49.9 0.6 %copy.9 = f32[8,128]{1,0:T(8,128)} copy(f32[8,128]{1,0:T(8,128)S(1)} %get-tuple-element.5) | data formatting | bytes 8192

commit v4 on v3

--- a/solution.py
+++ b/solution.py
@@ -22,7 +22,8 @@
 NEG = -1e6
 KV_ROWS = 4 * RUN
 Q_ROWS = 2 * GROUP * RUN
-META = 16
+META = 8
+TAIL = 16
 CHUNKS = (
     (("OO", 0), ("OX", 0), ("OO", -1), ("OO", 1)),
     (("OX", -1), ("OX", 1), ("OO", -2), ("OO", 2)),
@@ -322,6 +323,7 @@
     hbm = pl.BlockSpec(memory_space=pltpu.HBM)
     state = pltpu.VMEM((NX, Q_ROWS, HD), F32)
     shared = pltpu.VMEM((NX, Q_ROWS + META, HD), BF16)
+    partial = pltpu.VMEM((NX, Q_ROWS + TAIL, HD), BF16)
     blocks = len(SLOT)
     inputs = (positions.reshape(1, TOK), queries, keys, values)
     return pl.pallas_call(
@@ -342,8 +344,8 @@
             pltpu.VMEM((KV_ROWS + META, HD), BF16),
             shared,
             pltpu.VMEM((Q_ROWS + META, HD), BF16),
-            shared,
-            shared,
+            partial,
+            partial,
             state,
             state,
             state,

time: 50.7 us -> 50.2 us (level)
  no operation moved by 1% of the time
where the time goes in v4:
time: 50.2 us; the launch traced here: 50.1 us
  Pallas kernels  48.1 us (96%)
  local copies, waits for them, and re-layouts  1.3 us (3%)
  between operations  0.64 us (1%)
    pallas_call x1, Pallas kernels, shards(): pl.pallas_call(kernel, name='ring_attention', out_shape=(jax.ShapeDtypeSt...  48.1 us
    unnamed x2, local copies, waits for them, and re-layouts  1.3 us

profile of v4, /device:TPU:1, one launch (start us, length us, event | category | flops | bytes accessed | tf_op | source)
XLA Modules:
  0.0 50.1 jit_solution(15287696458705898939)
XLA Ops:
  0.6 48.1 %ring_attention.1 = (bf16[128,1024]{1,0:T(8,128)(2,1)S(1)}, f32[8,128]{1,0:T(8,128)S(1)}) custom-call(s32[1,128]{1,0:T(1,128)} %bitcast.1, bf16[128,1024]{1,0:T(8,128)(2,1)} %q_hbm.1, bf16[128,256]{1,0:T(8,128)(2,1)} %k_hbm.1, bf16[128,256]{1,0:T(8,128)(2,1)} %v_hbm.1), custom_call_target="tpu_custom_call" | custom-call | tf_op jit(solution)/shard_map/ring_attention/pallas_call | solution.py:329
  48.8 0.7 %copy.8 = bf16[128,1024]{1,0:T(8,128)(2,1)} copy(bf16[128,1024]{1,0:T(8,128)(2,1)S(1)} %get-tuple-element.4) | data formatting | bytes 524288
  49.5 0.6 %copy.9 = f32[8,128]{1,0:T(8,128)} copy(f32[8,128]{1,0:T(8,128)S(1)} %get-tuple-element.5) | data formatting | bytes 8192

commit v5 on v4

--- a/solution.py
+++ b/solution.py
@@ -42,8 +42,8 @@
     ("pass", "OO", 2), ("pass", "OX", 2),
     ("pass", "ZO", 0), ("pass", "ZX", 0), ("query",), ("wait", "OX", 0), ("attend", 0), ("attend", 1),
     ("pass", "OO", 3), ("pass", "OX", 3),
-    ("pass", "ZO", 1), ("pass", "ZX", 1), ("attend", 2),
-    ("far", "OO"), ("far", "OX"), ("attend", 3),
+    ("pass", "ZO", 1), ("pass", "ZX", 1),
+    ("far", "OO"), ("far", "OX"), ("attend", 2), ("attend", 3),
     ("pass", "ZO", 2), ("pass", "ZX", 2), ("attend", 4), ("attend", 5), ("attend", 6),
     ("wait", "ZO", 3), ("wait", "ZX", 3), ("wait", "ZO", 4), ("wait", "ZX", 4),
 )

time: 50.2 us -> 50.1 us (level)
  the two profiles are of different devices: /device:TPU:1 before, /device:TPU:16 now
where the time goes in v5:
time: 50.1 us; the launch traced here: 50 us
  Pallas kernels  48 us (96%)
  local copies, waits for them, and re-layouts  1.3 us (3%)
  between operations  0.64 us (1%)
    pallas_call x1, Pallas kernels, shards(): pl.pallas_call(kernel, name='ring_attention', out_shape=(jax.ShapeDtypeSt...  48 us
    unnamed x2, local copies, waits for them, and re-layouts  1.3 us

profile of v5, /device:TPU:16, one launch (start us, length us, event | category | flops | bytes accessed | tf_op | source)
XLA Modules:
  0.0 50.0 jit_solution(15544471721181803607)
XLA Ops:
  0.6 48.0 %ring_attention.1 = (bf16[128,1024]{1,0:T(8,128)(2,1)S(1)}, f32[8,128]{1,0:T(8,128)S(1)}) custom-call(s32[1,128]{1,0:T(1,128)} %bitcast.1, bf16[128,1024]{1,0:T(8,128)(2,1)} %q_hbm.1, bf16[128,256]{1,0:T(8,128)(2,1)} %k_hbm.1, bf16[128,256]{1,0:T(8,128)(2,1)} %v_hbm.1), custom_call_target="tpu_custom_call" | custom-call | tf_op jit(solution)/shard_map/ring_attention/pallas_call | solution.py:329
  48.7 0.7 %copy.8 = bf16[128,1024]{1,0:T(8,128)(2,1)} copy(bf16[128,1024]{1,0:T(8,128)(2,1)S(1)} %get-tuple-element.4) | data formatting | bytes 524288
  49.4 0.6 %copy.9 = f32[8,128]{1,0:T(8,128)} copy(f32[8,128]{1,0:T(8,128)S(1)} %get-tuple-element.5) | data formatting | bytes 8192
